TPU v7x, 32 devices: a whole 2x2x4 slice. The times are simulated.
32 devices in a mesh: rep: 4 (over x, core), shard: 8 (over z, y).
Axes of the slice: x: 2, y: 2, z: 4, core: 2. Of those that a mesh axis runs over, the one named last changes fastest.
Arguments:
- tokens: bfloat16 [32768, 768], P(('rep', 'shard')), may hold values from -6 to 6
- segment_ids: int32 [32, 1024], P(('rep', 'shard')), may hold values from 0 to 3, never falling along the last dimension, each value on 1 to 768 neighbouring positions
- norm1_gain: bfloat16 [768], P('shard'), may hold values from 0.5 to 1.5
- norm1_shift: bfloat16 [768], P('shard'), may hold values from -1.75 to 1.75
- w_qkv: bfloat16 [768, 2304], P('shard'), may hold values from -0.21875 to 0.21875
- q_bias: bfloat16 [768], P('shard'), may hold values from -3 to 3
- v_bias: bfloat16 [768], P('shard'), may hold values from -3 to 3
- w_out: bfloat16 [768, 768], P('shard'), may hold values from -0.875 to 0.875
- out_bias: bfloat16 [768], P('shard'), may hold values from -3 to 3
- norm2_gain: bfloat16 [768], P('shard'), may hold values from 0.5 to 1.5
- norm2_shift: bfloat16 [768], P('shard'), may hold values from -1.75 to 1.75
- w_fc: bfloat16 [768, 3072], P('shard'), may hold values from -0.21875 to 0.21875
- fc_bias: bfloat16 [3072], P('shard'), may hold values from -3 to 3
- w_proj: bfloat16 [3072, 768], P('shard'), may hold values from -0.109375 to 0.109375
- proj_bias: bfloat16 [768], P('shard'), may hold values from -3 to 3
- cotangent: bfloat16 [32768, 768], P(('rep', 'shard')), may hold values from -6 to 6
Outputs:
- layer_out: bfloat16 [32768, 768], P(('rep', 'shard'))
- grad_tokens: bfloat16 [32768, 768], P(('rep', 'shard'))
- grad_norm1_gain: float32 [768], P('shard')
- grad_norm1_shift: float32 [768], P('shard')
- grad_w_qkv: float32 [768, 2304], P('shard')
- grad_q_bias: float32 [768], P('shard')
- grad_v_bias: float32 [768], P('shard')
- grad_w_out: float32 [768, 768], P('shard')
- grad_out_bias: float32 [768], P('shard')
- grad_norm2_gain: float32 [768], P('shard')
- grad_norm2_shift: float32 [768], P('shard')
- grad_w_fc: float32 [768, 3072], P('shard')
- grad_fc_bias: float32 [3072], P('shard')
- grad_w_proj: float32 [3072, 768], P('shard')
- grad_proj_bias: float32 [768], P('shard')
All inputs are finite; a program needn't handle non-finite values.
Results may differ from a plain program's by a relative error of at most 0.014.
Values may be sent and summed in bfloat16 or wider, within the bound.
A program may use at most 320 MiB of HBM per device.

v0:
```python
from functools import partial

import jax
import jax.numpy as jnp
from jax import lax
from jax.sharding import PartitionSpec as P

HEAD = 64


EPSILON = 1e-05


def layer_norm(values, norm_gain, norm_shift):
    row_mean = jnp.mean(values, axis=-1, keepdims=True)
    centred = values - row_mean
    row_var = jnp.mean(centred * centred, axis=-1, keepdims=True)
    return centred * lax.rsqrt(row_var + EPSILON) * norm_gain + norm_shift


def block_mask(segment, block_start, block_size):
    position = jnp.arange(segment.shape[0])
    seg_block = lax.dynamic_slice_in_dim(segment, block_start, block_size)
    pos_block = lax.dynamic_slice_in_dim(position, block_start, block_size)
    return (seg_block[:, None] == segment[None, :]) & (position[None, :] <= pos_block[:, None])


def block_scores(q_block, key_rows, allowed):
    scale_by = q_block.shape[-1] ** (-0.5)
    scores = (
        jnp.einsum("qhd,khd->hqk", q_block, key_rows, preferred_element_type=jnp.float32) * scale_by
    )
    return jnp.where(allowed[None], scores, -1e30)


def attend_forward(pieces):
    queries, key_rows, value_rows, segment = pieces
    length = queries.shape[0]
    block_size = min(length, 512)
    out_blocks = []
    lse_blocks = []
    for block_start in range(0, length, block_size):
        q_block = queries[block_start : block_start + block_size]
        scores = block_scores(q_block, key_rows, block_mask(segment, block_start, block_size))
        row_max = jnp.max(scores, axis=-1, keepdims=True)
        exp_terms = jnp.exp(scores - row_max)
        row_total = jnp.sum(exp_terms, axis=-1, keepdims=True)
        probs_low = (exp_terms / row_total).astype(jnp.bfloat16)
        out_blocks.append(
            jnp.einsum(
                "hqk,khd->qhd", probs_low, value_rows, preferred_element_type=jnp.float32
            ).astype(jnp.bfloat16)
        )
        lse_blocks.append((row_max + jnp.log(row_total))[..., 0])
    return (jnp.concatenate(out_blocks, 0), jnp.concatenate(lse_blocks, 1))


def attend_backward(pieces):
    queries, key_rows, value_rows, segment, grad_mixed, log_totals = pieces
    length = queries.shape[0]
    block_size = min(length, 512)
    scale_by = queries.shape[-1] ** (-0.5)
    grad_keys = jnp.zeros(key_rows.shape, jnp.float32)
    grad_values = jnp.zeros(value_rows.shape, jnp.float32)
    query_blocks = []
    for block_start in range(0, length, block_size):
        q_block = queries[block_start : block_start + block_size]
        g_block = grad_mixed[block_start : block_start + block_size]
        scores = block_scores(q_block, key_rows, block_mask(segment, block_start, block_size))
        probs = jnp.exp(scores - log_totals[:, block_start : block_start + block_size, None])
        grad_probs = jnp.einsum(
            "qhd,khd->hqk", g_block, value_rows, preferred_element_type=jnp.float32
        )
        row_dot = jnp.sum(probs * grad_probs, axis=-1, keepdims=True)
        grad_scores = (probs * (grad_probs - row_dot)).astype(jnp.bfloat16)
        query_blocks.append(
            jnp.einsum("hqk,khd->qhd", grad_scores, key_rows, preferred_element_type=jnp.float32)
            * scale_by
        )
        grad_keys = (
            grad_keys
            + jnp.einsum("hqk,qhd->khd", grad_scores, q_block, preferred_element_type=jnp.float32)
            * scale_by
        )
        grad_values = grad_values + jnp.einsum(
            "hqk,qhd->khd", probs.astype(jnp.bfloat16), g_block, preferred_element_type=jnp.float32
        )
    return (jnp.concatenate(query_blocks, 0), grad_keys, grad_values)


def column_sums(values):
    return jnp.sum(values.astype(jnp.float32), axis=0)


def on_device(
    tokens,
    segment_ids,
    norm1_gain,
    norm1_shift,
    w_qkv,
    q_bias,
    v_bias,
    w_out,
    out_bias,
    norm2_gain,
    norm2_shift,
    w_fc,
    fc_bias,
    w_proj,
    proj_bias,
    cotangent,
):
    gathered = (
        lax.all_gather(norm1_gain, "shard", axis=0, tiled=True),
        lax.all_gather(norm1_shift, "shard", axis=0, tiled=True),
        lax.all_gather(w_qkv, "shard", axis=0, tiled=True),
        lax.all_gather(q_bias, "shard", axis=0, tiled=True),
        lax.all_gather(v_bias, "shard", axis=0, tiled=True),
        lax.all_gather(w_out, "shard", axis=0, tiled=True),
        lax.all_gather(out_bias, "shard", axis=0, tiled=True),
        lax.all_gather(norm2_gain, "shard", axis=0, tiled=True),
        lax.all_gather(norm2_shift, "shard", axis=0, tiled=True),
        lax.all_gather(w_fc, "shard", axis=0, tiled=True),
        lax.all_gather(fc_bias, "shard", axis=0, tiled=True),
        lax.all_gather(w_proj, "shard", axis=0, tiled=True),
        lax.all_gather(proj_bias, "shard", axis=0, tiled=True),
    )
    (
        full_g1,
        full_b1,
        full_qkv,
        full_bq,
        full_bv,
        full_wout,
        full_bout,
        full_g2,
        full_b2,
        full_wfc,
        full_bfc,
        full_wproj,
        full_bproj,
    ) = gathered
    seq_count, length = segment_ids.shape
    width = tokens.shape[1]
    head_count = width // HEAD
    tok_float = tokens.astype(jnp.float32)
    normed1, norm1_pull = jax.vjp(
        layer_norm, tok_float, full_g1.astype(jnp.float32), full_b1.astype(jnp.float32)
    )
    normed1_low = normed1.astype(jnp.bfloat16)
    qkv_bias = jnp.concatenate([full_bq, jnp.zeros_like(full_bq), full_bv]).astype(jnp.float32)
    projected = (
        jnp.dot(normed1_low, full_qkv, preferred_element_type=jnp.float32) + qkv_bias
    ).astype(jnp.bfloat16)
    projected = projected.reshape(seq_count, length, 3, head_count, HEAD)
    queries = projected[:, :, 0]
    key_rows = projected[:, :, 1]
    value_rows = projected[:, :, 2]
    attended, log_totals = lax.map(attend_forward, (queries, key_rows, value_rows, segment_ids))
    attended = attended.reshape(-1, width)
    middle = (
        tok_float
        + jnp.dot(attended, full_wout, preferred_element_type=jnp.float32)
        + full_bout.astype(jnp.float32)
    )
    normed2, norm2_pull = jax.vjp(
        layer_norm, middle, full_g2.astype(jnp.float32), full_b2.astype(jnp.float32)
    )
    normed2_low = normed2.astype(jnp.bfloat16)
    preact = jnp.dot(normed2_low, full_wfc, preferred_element_type=jnp.float32) + full_bfc.astype(
        jnp.float32
    )
    activated, gelu_pull = jax.vjp(partial(jax.nn.gelu, approximate=True), preact)
    activated_low = activated.astype(jnp.bfloat16)
    layer_out = (
        middle
        + jnp.dot(activated_low, full_wproj, preferred_element_type=jnp.float32)
        + full_bproj.astype(jnp.float32)
    ).astype(jnp.bfloat16)
    regathered = (
        lax.all_gather(norm1_gain, "shard", axis=0, tiled=True),
        lax.all_gather(norm1_shift, "shard", axis=0, tiled=True),
        lax.all_gather(w_qkv, "shard", axis=0, tiled=True),
        lax.all_gather(q_bias, "shard", axis=0, tiled=True),
        lax.all_gather(v_bias, "shard", axis=0, tiled=True),
        lax.all_gather(w_out, "shard", axis=0, tiled=True),
        lax.all_gather(out_bias, "shard", axis=0, tiled=True),
        lax.all_gather(norm2_gain, "shard", axis=0, tiled=True),
        lax.all_gather(norm2_shift, "shard", axis=0, tiled=True),
        lax.all_gather(w_fc, "shard", axis=0, tiled=True),
        lax.all_gather(fc_bias, "shard", axis=0, tiled=True),
        lax.all_gather(w_proj, "shard", axis=0, tiled=True),
        lax.all_gather(proj_bias, "shard", axis=0, tiled=True),
    )
    full_qkv = regathered[2]
    full_wout = regathered[5]
    full_wfc = regathered[9]
    full_wproj = regathered[11]
    grad_w_proj = jnp.einsum(
        "tk,tn->kn", activated_low, cotangent, preferred_element_type=jnp.float32
    )
    grad_proj_bias = column_sums(cotangent)
    grad_act = jnp.einsum("tn,kn->tk", cotangent, full_wproj, preferred_element_type=jnp.float32)
    grad_preact = gelu_pull(grad_act)[0].astype(jnp.bfloat16)
    grad_w_fc = jnp.einsum(
        "td,tk->dk", normed2_low, grad_preact, preferred_element_type=jnp.float32
    )
    grad_fc_bias = column_sums(grad_preact)
    grad_normed2 = jnp.einsum(
        "tk,dk->td", grad_preact, full_wfc, preferred_element_type=jnp.float32
    )
    grad_mid_norm, grad_norm2_gain, grad_norm2_shift = norm2_pull(grad_normed2)
    grad_middle = cotangent.astype(jnp.float32) + grad_mid_norm
    grad_branch = grad_middle.astype(jnp.bfloat16)
    grad_w_out = jnp.einsum("td,te->de", attended, grad_branch, preferred_element_type=jnp.float32)
    grad_out_bias = jnp.sum(grad_middle, axis=0)
    grad_attended = jnp.einsum(
        "te,de->td", grad_branch, full_wout, preferred_element_type=jnp.float32
    )
    grad_attended = grad_attended.astype(jnp.bfloat16).reshape(seq_count, length, head_count, HEAD)
    grad_queries, grad_keys, grad_values = lax.map(
        attend_backward, (queries, key_rows, value_rows, segment_ids, grad_attended, log_totals)
    )
    grad_projected = jnp.stack([grad_queries, grad_keys, grad_values], axis=2)
    grad_projected = grad_projected.astype(jnp.bfloat16).reshape(-1, 3 * width)
    grad_w_qkv = jnp.einsum(
        "td,tk->dk", normed1_low, grad_projected, preferred_element_type=jnp.float32
    )
    bias_sums = column_sums(grad_projected)
    grad_q_bias = bias_sums[:width]
    grad_v_bias = bias_sums[2 * width :]
    grad_normed1 = jnp.einsum(
        "tk,dk->td", grad_projected, full_qkv, preferred_element_type=jnp.float32
    )
    grad_tok_norm, grad_norm1_gain, grad_norm1_shift = norm1_pull(grad_normed1)
    grad_tokens = (grad_middle + grad_tok_norm).astype(jnp.bfloat16)
    (
        own_g1,
        own_b1,
        own_qkv,
        own_bq,
        own_bv,
        own_wout,
        own_bout,
        own_g2,
        own_b2,
        own_wfc,
        own_bfc,
        own_wproj,
        own_bproj,
    ) = (
        lax.psum_scatter(grad_norm1_gain, "shard", scatter_dimension=0, tiled=True),
        lax.psum_scatter(grad_norm1_shift, "shard", scatter_dimension=0, tiled=True),
        lax.psum_scatter(grad_w_qkv, "shard", scatter_dimension=0, tiled=True),
        lax.psum_scatter(grad_q_bias, "shard", scatter_dimension=0, tiled=True),
        lax.psum_scatter(grad_v_bias, "shard", scatter_dimension=0, tiled=True),
        lax.psum_scatter(grad_w_out, "shard", scatter_dimension=0, tiled=True),
        lax.psum_scatter(grad_out_bias, "shard", scatter_dimension=0, tiled=True),
        lax.psum_scatter(grad_norm2_gain, "shard", scatter_dimension=0, tiled=True),
        lax.psum_scatter(grad_norm2_shift, "shard", scatter_dimension=0, tiled=True),
        lax.psum_scatter(grad_w_fc, "shard", scatter_dimension=0, tiled=True),
        lax.psum_scatter(grad_fc_bias, "shard", scatter_dimension=0, tiled=True),
        lax.psum_scatter(grad_w_proj, "shard", scatter_dimension=0, tiled=True),
        lax.psum_scatter(grad_proj_bias, "shard", scatter_dimension=0, tiled=True),
    )
    summed = (
        lax.psum(own_g1.astype(jnp.bfloat16), "rep").astype(jnp.float32),
        lax.psum(own_b1.astype(jnp.bfloat16), "rep").astype(jnp.float32),
        lax.psum(own_qkv.astype(jnp.bfloat16), "rep").astype(jnp.float32),
        lax.psum(own_bq.astype(jnp.bfloat16), "rep").astype(jnp.float32),
        lax.psum(own_bv.astype(jnp.bfloat16), "rep").astype(jnp.float32),
        lax.psum(own_wout.astype(jnp.bfloat16), "rep").astype(jnp.float32),
        lax.psum(own_bout.astype(jnp.bfloat16), "rep").astype(jnp.float32),
        lax.psum(own_g2.astype(jnp.bfloat16), "rep").astype(jnp.float32),
        lax.psum(own_b2.astype(jnp.bfloat16), "rep").astype(jnp.float32),
        lax.psum(own_wfc.astype(jnp.bfloat16), "rep").astype(jnp.float32),
        lax.psum(own_bfc.astype(jnp.bfloat16), "rep").astype(jnp.float32),
        lax.psum(own_wproj.astype(jnp.bfloat16), "rep").astype(jnp.float32),
        lax.psum(own_bproj.astype(jnp.bfloat16), "rep").astype(jnp.float32),
    )
    return (
        layer_out,
        grad_tokens,
        summed[0],
        summed[1],
        summed[2],
        summed[3],
        summed[4],
        summed[5],
        summed[6],
        summed[7],
        summed[8],
        summed[9],
        summed[10],
        summed[11],
        summed[12],
    )


def solution(mesh):
    in_specs = (
        P(("rep", "shard"), None),
        P(("rep", "shard"), None),
        P("shard"),
        P("shard"),
        P("shard", None),
        P("shard"),
        P("shard"),
        P("shard", None),
        P("shard"),
        P("shard"),
        P("shard"),
        P("shard", None),
        P("shard"),
        P("shard", None),
        P("shard"),
        P(("rep", "shard"), None),
    )
    out_specs = (
        P(("rep", "shard"), None),
        P(("rep", "shard"), None),
        P("shard"),
        P("shard"),
        P("shard", None),
        P("shard"),
        P("shard"),
        P("shard", None),
        P("shard"),
        P("shard"),
        P("shard"),
        P("shard", None),
        P("shard"),
        P("shard", None),
        P("shard"),
    )
    return jax.shard_map(
        on_device, mesh=mesh, in_specs=in_specs, out_specs=out_specs, check_vma=False
    )
```

profile of v0, /device:TPU:0, one launch (start us, length us, event | category | flops | bytes accessed | tf_op | source)
XLA Modules:
  0.0 1029.0 jit_solution(10459978053637112987)
XLA Ops:
  19.4 39.5 %all-reduce.18 = (bf16[768]{0:T(1024)(128)(2,1)S(1)}, bf16[768]{0:T(1024)(128)(2,1)S(1)}, bf16[768]{0:T(1024)(128)(2,1)S(1)}, bf16[768]{0:T(1024)(128)(2,1)S(1)}...) all-reduce(bf16[768]{0:T(1024)(128)(2,1)S(1)} %dynamic-update-slice, ...), channel_id=1, replica_groups=mesh['rep'=4,'shard'=8] {'shard'}, use_global_device_ids=true, to_apply=%add.3 | all-reduce | flops 6144 | bytes 24576
  60.9 26.1 %all-gather = bf16[8,1,384]{2,1,0:T(2,128)(2,1)S(1)} all-gather(bf16[1,1,384]{2,1,0:T(2,128)(2,1)S(1)} %reshape.348), channel_id=1, replica_groups=mesh['rep'=4,'shard'=8] {'shard'}, dimensions={0}, use_global_device_ids=true | all-gather | bytes 6912 | tf_op jit(solution)/shard_map/all_gather | solution.py:124
  93.6 8.0 add_convert_fusion
  101.6 6.7 copy.55
  108.3 14.5 %fusion.20 = (f32[12,512]{1,0:T(8,128)S(1)}, f32[12,512,1024]{2,1,0:T(8,128)}) fusion(pred[512,1024]{1,0:T(8,128)(4,1)} %get-tuple-element.157, bf16[1,1024,3,12,64]{1,4,3,2,0:T(8,128)(2,1)} %bitcast.87), kind=kOutput, calls=%fused_computation.37 | convolution fusion | flops 824174592 | bytes 28073984 | tf_op jit(solution)/shard_map/while/body/eval_jaxpr/qhd,khd->hqk/dot_general | solution.py:31
  122.8 12.6 %fusion.1 = f32[12,512]{1,0:T(8,128)S(1)} fusion(f32[12,512]{1,0:T(8,128)S(1)} %get-tuple-element.162, f32[12,512,1024]{2,1,0:T(8,128)} %get-tuple-element.163, pred[512,1024]{1,0:T(8,128)(4,1)} %get-tuple-element.157), kind=kLoop, calls=%fused_computation.13 | loop fusion | flops 25159680 | bytes 25739264 | tf_op jit(solution)/shard_map/while/body/eval_jaxpr/reduce_sum | solution.py:47
  139.3 10.0 fusion.40
  149.3 11.2 %fusion.19 = (f32[12,512]{1,0:T(8,128)S(1)}, f32[12,512,1024]{2,1,0:T(8,128)}) fusion(pred[512,1024]{1,0:T(8,128)(4,1)S(1)} %get-tuple-element.156, bf16[1,1024,3,12,64]{1,4,3,2,0:T(8,128)(2,1)S(1)} %bitcast.93), kind=kOutput, calls=%fused_computation.36 | convolution fusion | flops 824174592 | bytes 28073984 | tf_op jit(solution)/shard_map/while/body/eval_jaxpr/qhd,khd->hqk/dot_general | solution.py:31
  160.6 13.0 %fusion = f32[12,512]{1,0:T(8,128)} fusion(f32[12,512]{1,0:T(8,128)S(1)} %get-tuple-element.164, f32[12,512,1024]{2,1,0:T(8,128)} %get-tuple-element.165, pred[512,1024]{1,0:T(8,128)(4,1)S(1)} %get-tuple-element.156), kind=kLoop, calls=%fused_computation.12 | loop fusion | flops 25159680 | bytes 25739264 | tf_op jit(solution)/shard_map/while/body/eval_jaxpr/reduce_sum | solution.py:47
  176.1 9.9 fusion.39
  193.1 8.4 all-gather.10.cloned.1.call-done
  201.5 10.5 %fusion.63 = f32[1024,3072]{1,0:T(8,128)} fusion(bf16[768,3072]{1,0:T(8,128)(2,1)} %all-gather.10.cloned.1.call-done, f32[1024,768]{0,1:T(8,128)S(1)} %get-tuple-element.167, f32[768]{0:T(1024)S(1)} %copy-done.27, f32[768]{0:T(1024)S(1)} %copy-done.26, f32[1024]{0:T(1024)S(1)} %fusion.50, f32[1024]{0:T(1024)S(1)} %broadcast_multiply_fusion), kind=kOutput, calls=%fused_computation.122 | convolution fusion | flops 4835770368 | bytes 20461568 | tf_op jit(solution)/shard_map/dot_general | solution.py:170
  212.1 69.6 %all-gather.12.cloned.1.call-done = bf16[3072,768]{1,0:T(8,128)(2,1)} async-done(((bf16[384,768]{1,0:T(8,128)(2,1)}), bf16[3072,768]{1,0:T(8,128)(2,1)}) %all-gather.12.cloned.1.call-update) | async-done | bytes 4718608 | tf_op jit(solution)/shard_map/all_gather | solution.py:125
  281.6 17.1 %convert_reduce_fusion = (f32[3072]{0:T(1024)}, bf16[1024,3072]{1,0:T(8,128)(2,1)S(1)}) fusion(f32[1024,3072]{1,0:T(8,128)} %fusion.63, f32[3072]{0:T(1024)S(1)} %bitcast.108, bf16[1024,768]{1,0:T(8,128)(2,1)} %param.31, bf16[3072,768]{1,0:T(8,128)(2,1)} %all-gather.12.cloned.1.call-done), kind=kOutput, calls=%fused_computation.27 | convolution fusion | flops 4904186880 | bytes 25190400 | tf_op jit(solution)/shard_map/tn,kn->tk/dot_general | solution.py:203
  298.8 7.4 fusion.72
  323.3 20.5 %multiply_reduce_fusion.1 = (f32[12,512]{1,0:T(8,128)S(1)}, f32[12,512,1024]{2,1,0:T(8,128)}) fusion(f32[12,512]{1,0:T(8,128)S(1)} %log_add_fusion.1, f32[12,512,1024]{2,1,0:T(8,128)} %get-tuple-element.165, pred[512,1024]{1,0:T(8,128)(4,1)S(1)} %copy-done.13, bf16[512,12,64]{0,2,1:T(8,128)(2,1)S(1)} %bitcast.101, bf16[1,1024,3,12,64]{1,4,3,2,0:T(8,128)(2,1)} %bitcast.88), kind=kOutput, calls=%fused_computation.4 | convolution fusion | flops 836757504 | bytes 53264384 | tf_op jit(solution)/shard_map/while/body/eval_jaxpr/qhd,khd->hqk/dot_general | solution.py:71
  343.8 18.5 %multiply_reduce_fusion = (f32[12,512]{1,0:T(8,128)S(1)}, f32[12,512,1024]{2,1,0:T(8,128)}) fusion(f32[12,512]{1,0:T(8,128)S(1)} %log_add_fusion, f32[12,512,1024]{2,1,0:T(8,128)} %get-tuple-element.163, pred[512,1024]{1,0:T(8,128)(4,1)S(1)} %copy-done.15, bf16[512,12,64]{0,2,1:T(8,128)(2,1)} %bitcast.103, bf16[1,1024,3,12,64]{1,4,3,2,0:T(8,128)(2,1)} %bitcast.89), kind=kOutput, calls=%fused_computation.1 | convolution fusion | flops 836757504 | bytes 53264384 | tf_op jit(solution)/shard_map/while/body/eval_jaxpr/qhd,khd->hqk/dot_general | solution.py:71
  362.3 42.6 %multiply_convert_fusion = (bf16[12,512,1024]{2,1,0:T(8,128)(2,1)}, bf16[12,512,1024]{2,1,0:T(8,128)(2,1)}) fusion(f32[12,512,1024]{2,1,0:T(8,128)} %get-tuple-element.171, f32[12,512]{1,0:T(8,128)S(1)} %get-tuple-element.170, f32[12,512]{1,0:T(8,128)S(1)} %log_add_fusion, f32[12,512,1024]{2,1,0:T(8,128)} %get-tuple-element.163, ...), kind=kLoop, calls=%fused_computation | loop fusion | flops 75497472 | bytes 126976000 | tf_op jit(solution)/shard_map/while/body/eval_jaxpr/convert_element_type | solution.py:75
  405.0 9.5 multiply_bitcast_fusion.2
  414.5 8.5 fusion.47
  423.1 9.1 multiply_bitcast_fusion.1
  432.2 7.4 multiply_bitcast_fusion
  439.9 11.9 %fusion.11 = f32[12,64,1024]{2,1,0:T(8,128)S(1)} fusion(bf16[512,12,64]{0,2,1:T(8,128)(2,1)S(1)} %bitcast.104, f32[12,512]{1,0:T(8,128)S(1)} %log_add_fusion, f32[12,512,1024]{2,1,0:T(8,128)} %get-tuple-element.163, pred[512,1024]{1,0:T(8,128)(4,1)S(1)} %copy-done.16), kind=kOutput, calls=%fused_computation.25 | convolution fusion | flops 830472192 | bytes 29646848 | tf_op jit(solution)/shard_map/while/body/eval_jaxpr/hqk,qhd->khd/dot_general | solution.py:85
  451.9 12.1 %add_bitcast_fusion = bf16[1,1024,1,12,64]{1,4,3,2,0:T(8,128)(2,1)S(1)} fusion(f32[12,64,1024]{2,1,0:T(8,128)S(1)} %fusion.11, bf16[512,12,64]{0,2,1:T(8,128)(2,1)S(1)} %bitcast.102, f32[12,512]{1,0:T(8,128)S(1)} %log_add_fusion.1, f32[12,512,1024]{2,1,0:T(8,128)} %get-tuple-element.165, pred[512,1024]{1,0:T(8,128)(4,1)S(1)} %copy-done.14), kind=kOutput, calls=%fused_computation.60 | convolution fusion | flops 832045056 | bytes 31219712 | tf_op jit(solution)/shard_map/while/body/eval_jaxpr/hqk,qhd->khd/dot_general | solution.py:85
  474.8 12.9 %fusion.64 = f32[3072,768]{1,0:T(8,128)} fusion(bf16[1024,768]{1,0:T(8,128)(2,1)S(1)} %copy-done.24, f32[1024,3072]{1,0:T(8,128)} %fusion.63, f32[3072]{0:T(1024)S(1)} %bitcast.109), kind=kOutput, calls=%fused_computation.123 | convolution fusion | flops 4863295488 | bytes 23605248 | tf_op jit(solution)/shard_map/tk,tn->kn/dot_general | solution.py:199
  488.4 10.7 %fusion.62 = f32[768,3072]{1,0:T(8,128)} fusion(bf16[1024,3072]{1,0:T(8,128)(2,1)} %copy-done.48, f32[1024,768]{0,1:T(8,128)} %copy-done.5, f32[768]{0:T(1024)S(1)} %copy-done.28, f32[768]{0:T(1024)S(1)} %copy-done.26, f32[1024]{0:T(1024)S(1)} %fusion.50, f32[1024]{0:T(1024)S(1)} %broadcast_multiply_fusion), kind=kOutput, calls=%fused_computation.121 | convolution fusion | flops 4835770368 | bytes 18888704 | tf_op jit(solution)/shard_map/td,tk->dk/dot_general | solution.py:205
  500.5 8.9 fusion.71
  518.9 11.8 %add_convert_fusion.2 = bf16[1024,768]{0,1:T(8,128)(2,1)} fusion(f32[1024,768]{0,1:T(8,128)S(1)} %copy-done.6, bf16[3072,768]{1,0:T(8,128)(2,1)} %all-gather.12.cloned.1.call-done, f32[768]{0:T(1024)S(1)} %convert_element_type.225, f32[1024,3072]{1,0:T(8,128)} %fusion.63, f32[3072]{0:T(1024)S(1)} %bitcast.110), kind=kOutput, calls=%fused_computation.63 | convolution fusion | flops 4865654784 | bytes 22035456 | tf_op jit(solution)/shard_map/dot_general | solution.py:177
  532.4 89.5 %reduce-scatter.5.cloned.1.call-done = f32[96,2304]{1,0:T(8,128)} async-done(((f32[768,2304]{1,0:T(8,128)}), f32[96,2304]{1,0:T(8,128)}) %reduce-scatter.5.cloned.1.call-update) | async-done | bytes 884752 | tf_op jit(solution)/shard_map/reduce_scatter | solution.py:254
  623.8 164.6 %reduce-scatter.11.cloned.1.call-done = f32[384,768]{1,0:T(8,128)} async-done(((f32[3072,768]{1,0:T(8,128)}), f32[384,768]{1,0:T(8,128)}) %reduce-scatter.11.cloned.1.call-update) | async-done | bytes 1179664 | tf_op jit(solution)/shard_map/reduce_scatter | solution.py:263
  790.6 164.4 %reduce-scatter.9.cloned.1.call-done = f32[96,3072]{1,0:T(8,128)} async-done(((f32[768,3072]{1,0:T(8,128)}), f32[96,3072]{1,0:T(8,128)}) %reduce-scatter.9.cloned.1.call-update) | async-done | bytes 1179664 | tf_op jit(solution)/shard_map/reduce_scatter | solution.py:261
  965.0 35.6 %all-reduce.17 = (bf16[768]{0:T(1024)(128)(2,1)S(1)}, bf16[768]{0:T(1024)(128)(2,1)S(1)}, bf16[768]{0:T(1024)(128)(2,1)S(1)}, bf16[768]{0:T(1024)(128)(2,1)S(1)}...) all-reduce(f32[768]{0:T(1024)S(1)} %get-tuple-element.113, ...), channel_id=2, replica_groups=mesh['rep'=4,'shard'=8] {'shard'}, use_global_device_ids=true, to_apply=%region_15.16.clone | all-reduce | flops 9216 | bytes 55296
  (221 shorter events, 109.0 us)
Async XLA Ops:
  7.2 82.9 %copy-start.23 = (bf16[1024,768]{1,0:T(8,128)(2,1)S(1)}, bf16[1024,768]{1,0:T(8,128)(2,1)}, u32[]{:S(2)}) copy-start(bf16[1024,768]{1,0:T(8,128)(2,1)} %param.31) | copy-start | bytes 4718596
  7.2 86.4 %all-gather.6.cloned.1.call-start = ((), (), s32[]{:S(2)}) async-start(), calls=%async_computation.4 | async-start | bytes 3981312 | tf_op jit(solution)/shard_map/all_gather | solution.py:116
  7.9 180.8 %all-gather.8.cloned.1.call-start = ((), (), s32[]{:S(2)}) async-start(), calls=%async_computation.5 | async-start | bytes 1327104 | tf_op jit(solution)/shard_map/all_gather | solution.py:119
  8.7 192.9 %all-gather.10.cloned.1.call-start = ((), (), s32[]{:S(2)}) async-start(), calls=%async_computation.6 | async-start | bytes 5308416 | tf_op jit(solution)/shard_map/all_gather | solution.py:123
  9.4 272.2 %all-gather.12.cloned.1.call-start = ((), (), s32[]{:S(2)}) async-start(), calls=%async_computation.7 | async-start | bytes 5308416 | tf_op jit(solution)/shard_map/all_gather | solution.py:125
  10.0 520.7 %reduce-scatter.7.cloned.1.call-start = ((), (), s32[]{:S(2)}) async-start(), calls=%async_computation.9 | async-start | bytes 2654208 | tf_op jit(solution)/shard_map/reduce_scatter | solution.py:257
  58.9 34.7 %copy-start.32 = (f32[768]{0:T(1024)}, f32[768]{0:T(1024)S(1)}, u32[]{:S(2)}) copy-start(f32[768]{0:T(1024)S(1)} %convert_element_type.208) | copy-start | bytes 9220
  59.5 34.1 %copy-start.44 = (f32[768]{0:T(1024)}, f32[768]{0:T(1024)S(1)}, u32[]{:S(2)}) copy-start(f32[768]{0:T(1024)S(1)} %convert_element_type.209) | copy-start | bytes 9220
  89.3 12.3 %copy-start.3 = (bf16[1024,768]{0,1:T(8,128)(2,1)}, bf16[1024,768]{0,1:T(8,128)(2,1)S(1)}, u32[]{:S(2)}) copy-start(bf16[1024,768]{0,1:T(8,128)(2,1)S(1)} %copy.54) | copy-start | bytes 4718596
  89.6 12.0 %copy-start.30 = (f32[1024]{0:T(1024)}, f32[1024]{0:T(1024)S(1)}, u32[]{:S(2)}) copy-start(f32[1024]{0:T(1024)S(1)} %broadcast_multiply_fusion.1) | copy-start | bytes 12292
  90.1 11.5 %copy-start.34 = (f32[1024]{0:T(1024)}, f32[1024]{0:T(1024)S(1)}, u32[]{:S(2)}) copy-start(f32[1024]{0:T(1024)S(1)} %fusion.49) | copy-start | bytes 12292
  93.6 79.9 %copy-start.12 = (pred[512,1024]{1,0:T(8,128)(4,1)}, pred[512,1024]{1,0:T(8,128)(4,1)S(1)}, u32[]{:S(2)}) copy-start(pred[512,1024]{1,0:T(8,128)(4,1)S(1)} %get-tuple-element.156) | copy-start | bytes 1572868
  108.3 27.1 %copy-start.2 = (bf16[1024,2304]{0,1:T(8,128)(2,1)S(1)}, bf16[1024,2304]{0,1:T(8,128)(2,1)}, u32[]{:S(2)}) copy-start(bf16[1024,2304]{0,1:T(8,128)(2,1)} %copy.55) | copy-start | bytes 14155780
  122.8 16.5 %copy-start = (f32[12,512,1024]{2,1,0:T(8,128)S(1)}, f32[12,512,1024]{2,1,0:T(8,128)}, u32[]{:S(2)}) copy-start(f32[12,512,1024]{2,1,0:T(8,128)} %get-tuple-element.163) | copy-start | bytes 75497472
  160.6 15.5 %copy-start.1 = (f32[12,512,1024]{2,1,0:T(8,128)S(1)}, f32[12,512,1024]{2,1,0:T(8,128)}, u32[]{:S(2)}) copy-start(f32[12,512,1024]{2,1,0:T(8,128)} %get-tuple-element.165) | copy-start | bytes 75497472
  188.8 12.8 %copy-start.26 = (f32[768]{0:T(1024)S(1)}, f32[768]{0:T(1024)}, u32[]{:S(2)}) copy-start(f32[768]{0:T(1024)} %convert_element_type.220) | copy-start | bytes 9220
  188.8 12.8 %copy-start.27 = (f32[768]{0:T(1024)S(1)}, f32[768]{0:T(1024)}, u32[]{:S(2)}) copy-start(f32[768]{0:T(1024)} %convert_element_type.221) | copy-start | bytes 9220
  192.6 120.6 %copy-start.5 = (f32[1024,768]{0,1:T(8,128)}, f32[1024,768]{0,1:T(8,128)S(1)}, u32[]{:S(2)}) copy-start(f32[1024,768]{0,1:T(8,128)S(1)} %get-tuple-element.167) | copy-start | bytes 9437188
  193.1 88.5 %copy-start.42 = (f32[8,1,384]{2,1,0:T(1,128)S(1)}, f32[8,1,384]{2,1,0:T(1,128)}, u32[]{:S(2)}) copy-start(f32[8,1,384]{2,1,0:T(1,128)} %convert_element_type.266) | copy-start | bytes 36868
  281.6 17.1 %copy-start.17 = (bf16[768,3072]{1,0:T(8,128)(2,1)S(1)}, bf16[768,3072]{1,0:T(8,128)(2,1)}, u32[]{:S(2)}) copy-start(bf16[768,3072]{1,0:T(8,128)(2,1)} %all-gather.10.cloned.1.call-done) | copy-start | bytes 14155780
  323.3 20.5 %copy-start.20 = (bf16[512,768]{0,1:T(8,128)(2,1)}, bf16[512,768]{0,1:T(8,128)(2,1)S(1)}, u32[]{:S(2)}) copy-start(bf16[512,768]{0,1:T(8,128)(2,1)S(1)} %get-tuple-element.152) | copy-start | bytes 2359300
  323.3 20.5 %copy-start.15 = (pred[512,1024]{1,0:T(8,128)(4,1)S(1)}, pred[512,1024]{1,0:T(8,128)(4,1)}, u32[]{:S(2)}) copy-start(pred[512,1024]{1,0:T(8,128)(4,1)} %get-tuple-element.157) | copy-start | bytes 1572868
  343.8 61.2 %slice-start = ((s8[4718592]{0:T(1024)(128)(4,1)}), s8[524288]{0:T(1024)(128)(4,1)S(1)}, s32[]{:S(2)}) async-start(s8[4718592]{0:T(1024)(128)(4,1)} %bitcast.95), calls=%async_computation.13 | async-start | bytes 1048576
  362.3 42.6 %slice-start.1 = ((s8[4718592]{0:T(1024)(128)(4,1)}), s8[4194304]{0:T(1024)(128)(4,1)S(1)}, s32[]{:S(2)}) async-start(s8[4718592]{0:T(1024)(128)(4,1)} %bitcast.95), calls=%async_computation.14 | async-start | bytes 8388608
  423.0 198.8 %reduce-scatter.5.cloned.1.call-start = ((), (), s32[]{:S(2)}) async-start(), calls=%async_computation.8 | async-start | bytes 7962624 | tf_op jit(solution)/shard_map/reduce_scatter | solution.py:254
  439.9 11.9 %copy-start.14 = (pred[512,1024]{1,0:T(8,128)(4,1)S(1)}, pred[512,1024]{1,0:T(8,128)(4,1)}, u32[]{:S(2)}) copy-start(pred[512,1024]{1,0:T(8,128)(4,1)} %copy-done.12) | copy-start | bytes 1572868
  439.9 11.9 %copy-start.21 = (bf16[512,768]{0,1:T(8,128)(2,1)S(1)}, bf16[512,768]{0,1:T(8,128)(2,1)}, u32[]{:S(2)}) copy-start(bf16[512,768]{0,1:T(8,128)(2,1)} %copy-done.20) | copy-start | bytes 2359300
  473.4 315.0 %reduce-scatter.11.cloned.1.call-start = ((), (), s32[]{:S(2)}) async-start(), calls=%async_computation.11 | async-start | bytes 10616832 | tf_op jit(solution)/shard_map/reduce_scatter | solution.py:263
  487.8 467.3 %reduce-scatter.9.cloned.1.call-start = ((), (), s32[]{:S(2)}) async-start(), calls=%async_computation.10 | async-start | bytes 10616832 | tf_op jit(solution)/shard_map/reduce_scatter | solution.py:261
  499.1 515.1 %all-reduce.23.cloned.1.call-start = ((), (), s32[]{:S(2)}) async-start(), calls=%async_computation.12 | async-start | bytes 3538944 | tf_op jit(solution)/shard_map/psum | solution.py:269
  532.4 427.6 %copy-start.11 = (bf16[1024,768]{0,1:T(8,128)(2,1)S(1)}, bf16[1024,768]{0,1:T(8,128)(2,1)}, u32[]{:S(2)}) copy-start(bf16[1024,768]{0,1:T(8,128)(2,1)} %copy.57) | copy-start | bytes 4718596
  532.4 427.6 %copy-start.39 = (f32[1024]{0:T(1024)S(1)}, f32[1024]{0:T(1024)}, u32[]{:S(2)}) copy-start(f32[1024]{0:T(1024)} %copy-done.38) | copy-start | bytes 12292
  (28 other events, 117.0 us)
Sparse Core Ops, SparseCore 0:
  10.2 68.4 all-gather.5
  80.9 39.7 all-gather.7
  122.8 78.6 all-gather.9
  203.6 78.0 all-gather.11
  423.1 67.0 reduce-scatter.6
  493.7 128.0 reduce-scatter.4
  625.9 162.5 reduce-scatter.10
  792.5 162.5 reduce-scatter.8
  959.0 45.7 all-reduce.22
where the time goes:
time: 1030 us
  waiting for transfers between devices  499 us (48%)
  matrix products  246 us (24%)
  other arithmetic  113 us (11%)
  blocking collectives  107 us (10%)
  local copies, waits for them, and re-layouts  46.3 us (4%)
  between operations  16.7 us (2%)
    reduce_scatter x1, waiting for transfers between devices, on_device(): lax.psum_scatter(grad_w_proj, 'shard', scatter_dimension=0, tiled=True)  165 us
    reduce_scatter x1, waiting for transfers between devices, on_device(): lax.psum_scatter(grad_w_fc, 'shard', scatter_dimension=0, tiled=True)  164 us
    reduce_scatter x1, waiting for transfers between devices, on_device(): lax.psum_scatter(grad_w_qkv, 'shard', scatter_dimension=0, tiled=True)  89.5 us
    unnamed x2, blocking collectives  75.1 us
    all_gather x1, waiting for transfers between devices, on_device(): lax.all_gather(w_proj, 'shard', axis=0, tiled=True)  69.6 us
    convert_element_type x1, other arithmetic, attend_backward(): grad_scores = (probs * (grad_probs - row_dot)).astype(jnp.bfloat16)  42.6 us
    dot_general x2, matrix products, attend_backward(): jnp.einsum('qhd,khd->hqk', g_block, value_rows, preferred_element_type=jn...  39 us
    unnamed x134, local copies, waits for them, and re-layouts  30.7 us
  transfers between devices with their start and end apart: 9, of which 5 were waited for; matrix products, arithmetic and copies ran while one was open for 24% of the time, Pallas kernels for 0%

commit v1 on v0

v1 whole, which is shorter than its diff:
```python
from functools import partial

import jax
import jax.numpy as jnp
from jax import lax
from jax.experimental import pallas as pl
from jax.experimental.pallas import tpu as pltpu
from jax.sharding import PartitionSpec as P

HEAD = 64
EPSILON = 1e-05
QUERY_BLOCK = 256
ROW_CHUNK = 256
MASKED = -1e30
GELU_SCALE = 0.7978845608028654
GELU_CUBE = 0.044715
VMEM_LIMIT = 62 << 20
NN = (((1,), (0,)), ((), ()))
NT = (((1,), (1,)), ((), ()))
f32 = jnp.float32
bf16 = jnp.bfloat16
WHOLE = pl.BlockSpec(memory_space=pltpu.VMEM)

GAIN1, SHIFT1, BIAS_Q, BIAS_V, BIAS_OUT, GAIN2, SHIFT2, BIAS_PROJ, BIAS_FC = range(9)


def matmul(left, right, dims):
    return lax.dot_general(left, right, dims, preferred_element_type=f32)


def normalized(values):
    centred = values - jnp.mean(values, axis=-1, keepdims=True)
    inverse = lax.rsqrt(jnp.mean(centred * centred, axis=-1, keepdims=True) + EPSILON)
    return centred * inverse, inverse


def norm_pull(grad_normed, gain_row, norm, inverse):
    scaled = grad_normed * gain_row
    return inverse * (
        scaled
        - jnp.mean(scaled, axis=-1, keepdims=True)
        - norm * jnp.mean(scaled * norm, axis=-1, keepdims=True)
    )


def total(values):
    return jnp.sum(values, axis=0, keepdims=True)


def block(index, size):
    return pl.ds(pl.multiple_of(index * size, size), size)


def build_mask(segment_ref, mask_ref):
    length = segment_ref.shape[1]
    query_seg = segment_ref[...].astype(f32)
    key_seg = jnp.transpose(jnp.broadcast_to(query_seg, (8, length)))[:, 0:1]
    for start in range(0, length, QUERY_BLOCK):
        stop = start + QUERY_BLOCK
        key_at = lax.broadcasted_iota(jnp.int32, (stop, QUERY_BLOCK), 0)
        query_at = lax.broadcasted_iota(jnp.int32, (stop, QUERY_BLOCK), 1) + start
        allowed = (key_seg[0:stop] == query_seg[:, start:stop]) & (key_at <= query_at)
        mask_ref[0:stop, start:stop] = jnp.where(allowed, 0.0, MASKED)


def half_lanes(which):
    lane = lax.broadcasted_iota(jnp.int32, (1, 2 * HEAD), 1)
    return (lane < HEAD) if which == 0 else (lane >= HEAD)


def keep_half(values, which):
    return jnp.where(half_lanes(which), values, jnp.zeros_like(values))


def attend_forward(pair, projected_ref, values_t_ref, mask_ref, attended_t_ref, lse_ref):
    length, width = projected_ref.shape[0], projected_ref.shape[1] // 3
    pairs = width // (2 * HEAD)
    queries = projected_ref[:, block(pair, 2 * HEAD)] * bf16(HEAD**-0.5)
    keys = projected_ref[:, block(pairs + pair, 2 * HEAD)]
    for which in range(2):
        head_queries = keep_half(queries, which)
        rows = block(2 * pair + which, HEAD)
        values_t = values_t_ref[rows, :]
        for start in range(0, length, QUERY_BLOCK):
            stop = start + QUERY_BLOCK
            scores = matmul(keys[0:stop], head_queries[start:stop], NT)
            scores = scores + mask_ref[0:stop, start:stop]
            top = jnp.max(scores, axis=0, keepdims=True)
            terms = jnp.exp(scores - top)
            sums = jnp.sum(terms, axis=0, keepdims=True)
            mixed = matmul(values_t[:, 0:stop], terms.astype(bf16), NN)
            attended_t_ref[rows, start:stop] = (mixed * (1.0 / sums)).astype(bf16)
            lse_ref[pl.ds(2 * pair + which, 1), start:stop] = top + jnp.log(sums)


def attend_backward(
    pair,
    projected_ref,
    keys_t_ref,
    grad_attended_ref,
    mask_ref,
    lse_ref,
    dots_ref,
    grad_queries_t_ref,
    grad_projected_ref,
    grad_keys_ref,
    grad_values_ref,
):
    length, width = projected_ref.shape[0], projected_ref.shape[1] // 3
    pairs = width // (2 * HEAD)
    scale_by = HEAD**-0.5
    queries = projected_ref[:, block(pair, 2 * HEAD)] * bf16(scale_by)
    keys = projected_ref[:, block(pairs + pair, 2 * HEAD)]
    values = projected_ref[:, block(2 * pairs + pair, 2 * HEAD)]
    grads = grad_attended_ref[:, block(pair, 2 * HEAD)]
    for start in reversed(range(0, length, QUERY_BLOCK)):
        stop = start + QUERY_BLOCK
        grad_keys = grad_values = 0.0
        for which in range(2):
            head = pl.ds(2 * pair + which, 1)
            rows = block(2 * pair + which, HEAD)
            query_rows = keep_half(queries[start:stop], which)
            grad_rows = keep_half(grads[start:stop], which)
            scores = matmul(keys[0:stop], query_rows, NT)
            probs = jnp.exp(scores + mask_ref[0:stop, start:stop] - lse_ref[head, start:stop])
            grad_probs = matmul(values[0:stop], grad_rows, NT)
            grad_scores = (probs * (grad_probs - dots_ref[head, start:stop])).astype(bf16)
            grad_values = grad_values + matmul(probs.astype(bf16), grad_rows, NN)
            grad_keys = grad_keys + matmul(grad_scores, query_rows, NN)
            grad_queries_t_ref[rows, start:stop] = (
                matmul(keys_t_ref[rows, 0:stop], grad_scores, NN) * scale_by
            )
        if stop == length:
            grad_keys_ref[...] = grad_keys
            grad_values_ref[...] = grad_values
        else:
            grad_keys_ref[0:stop] += grad_keys
            grad_values_ref[0:stop] += grad_values
    grad_projected_ref[:, block(pairs + pair, 2 * HEAD)] = grad_keys_ref[...].astype(bf16)
    grad_projected_ref[:, block(2 * pairs + pair, 2 * HEAD)] = grad_values_ref[...].astype(bf16)


def forward_kernel(
    tokens_ref,
    segment_ref,
    params_ref,
    w_qkv_ref,
    projected_ref,
    attended_t_ref,
    lse_ref,
    mask_ref,
    normed_ref,
    values_t_ref,
):
    length, width = tokens_ref.shape
    row = lambda at: params_ref[at : at + 1, :]
    for at in range(0, length, ROW_CHUNK):
        norm, _ = normalized(tokens_ref[at : at + ROW_CHUNK].astype(f32))
        normed_ref[at : at + ROW_CHUNK] = (norm * row(GAIN1) + row(SHIFT1)).astype(bf16)
    for part, bias in enumerate((row(BIAS_Q), 0.0, row(BIAS_V))):
        columns = slice(part * width, (part + 1) * width)
        projected_ref[:, columns] = (
            matmul(normed_ref[...], w_qkv_ref[:, columns], NN) + bias
        ).astype(bf16)
    build_mask(segment_ref, mask_ref)
    values_t_ref[...] = jnp.transpose(projected_ref[:, 2 * width :])

    @pl.loop(0, width // (2 * HEAD))
    def _(pair):
        attend_forward(pair, projected_ref, values_t_ref, mask_ref, attended_t_ref, lse_ref)


def hidden_kernel(
    attended_t_ref,
    tokens_ref,
    cotangent_ref,
    params_ref,
    w_out_ref,
    w_fc_ref,
    w_proj_ref,
    layer_out_ref,
    grad_middle_ref,
    grad_attended_ref,
    grad_w_out_ref,
    grad_w_fc_ref,
    grad_w_proj_t_ref,
    small_ref,
    middle_ref,
    normed_ref,
    normed_t_ref,
    cotangent_t_ref,
    mixed_ref,
    grad_normed_ref,
    activated_ref,
    grad_preact_ref,
):
    step, steps = pl.program_id(0), pl.num_programs(0)
    length, width = tokens_ref.shape
    row = lambda at: params_ref[at : at + 1, :]
    chunks = [slice(at, at + ROW_CHUNK) for at in range(0, length, ROW_CHUNK)]

    @pl.when(step == 0)
    def _():
        attended = jnp.transpose(attended_t_ref[...])
        middle_ref[...] = (
            tokens_ref[...].astype(f32) + matmul(attended, w_out_ref[...], NN) + row(BIAS_OUT)
        )
        for rows in chunks:
            norm, _ = normalized(middle_ref[rows])
            normed_ref[rows] = (norm * row(GAIN2) + row(SHIFT2)).astype(bf16)
        normed_t_ref[...] = jnp.transpose(normed_ref[...])
        cotangent_t_ref[...] = jnp.transpose(cotangent_ref[...])
        mixed_ref[...] = jnp.zeros_like(mixed_ref)
        grad_normed_ref[...] = jnp.zeros_like(grad_normed_ref)
        small_ref[...] = jnp.zeros_like(small_ref)

    bias_sum = 0.0
    bias_row = params_ref[pl.ds(BIAS_FC + step, 1), :]
    for rows in chunks:
        preact = matmul(normed_ref[rows], w_fc_ref[...], NN) + bias_row
        grad_act = matmul(cotangent_ref[rows], w_proj_ref[...], NT)
        square = preact * preact
        bend = jnp.tanh(GELU_SCALE * preact * (1.0 + GELU_CUBE * square))
        gate = 0.5 + 0.5 * bend
        activated_ref[rows] = (preact * gate).astype(bf16)
        slope = gate + (0.5 * GELU_SCALE) * preact * (1.0 - bend * bend) * (
            1.0 + (3 * GELU_CUBE) * square
        )
        grad_preact = (slope * grad_act).astype(bf16)
        grad_preact_ref[rows] = grad_preact
        bias_sum = bias_sum + total(grad_preact.astype(f32))
    small_ref[pl.ds(BIAS_FC + step, 1), :] = bias_sum
    mixed_ref[...] += matmul(activated_ref[...], w_proj_ref[...], NN)
    grad_w_proj_t_ref[...] = matmul(cotangent_t_ref[...], activated_ref[...], NN).astype(bf16)
    grad_w_fc_ref[...] = matmul(normed_t_ref[...], grad_preact_ref[...], NN).astype(bf16)
    grad_normed_ref[...] += matmul(grad_preact_ref[...], w_fc_ref[...], NT)

    @pl.when(step == steps - 1)
    def _():
        sums = [0.0] * 4
        for rows in chunks:
            middle = middle_ref[rows]
            layer_out_ref[rows] = (middle + mixed_ref[rows] + row(BIAS_PROJ)).astype(bf16)
            norm, inverse = normalized(middle)
            grad_normed = grad_normed_ref[rows]
            cotangent = cotangent_ref[rows].astype(f32)
            grad_middle = cotangent + norm_pull(grad_normed, row(GAIN2), norm, inverse)
            grad_middle_ref[rows] = grad_middle
            normed_ref[rows] = grad_middle.astype(bf16)
            terms = (grad_middle, grad_normed * norm, grad_normed, cotangent)
            sums = [a + total(b) for a, b in zip(sums, terms)]
        for at, value in zip((BIAS_OUT, GAIN2, SHIFT2, BIAS_PROJ), sums):
            small_ref[at : at + 1, :] = value
        grad_branch = normed_ref[...]
        grad_w_out_ref[...] = matmul(attended_t_ref[...], grad_branch, NN).astype(bf16)
        grad_attended_ref[...] = matmul(grad_branch, w_out_ref[...], NT).astype(bf16)


def backward_kernel(
    tokens_ref,
    segment_ref,
    params_ref,
    w_qkv_ref,
    projected_ref,
    attended_t_ref,
    lse_ref,
    grad_attended_ref,
    grad_middle_ref,
    small_in_ref,
    grad_tokens_ref,
    grad_w_qkv_ref,
    small_ref,
    mask_ref,
    wide_t_ref,
    grad_queries_t_ref,
    dots_ref,
    grad_projected_ref,
    grad_keys_ref,
    grad_values_ref,
):
    length, width = tokens_ref.shape
    row = lambda at: params_ref[at : at + 1, :]
    build_mask(segment_ref, mask_ref)
    wide_t_ref[...] = jnp.transpose(grad_attended_ref[...])
    for head in range(width // HEAD):
        rows = slice(head * HEAD, (head + 1) * HEAD)
        dots_ref[head : head + 1, :] = total(
            wide_t_ref[rows].astype(f32) * attended_t_ref[rows].astype(f32)
        )
    wide_t_ref[...] = jnp.transpose(projected_ref[:, width : 2 * width])

    @pl.loop(0, width // (2 * HEAD))
    def _(pair):
        attend_backward(
            pair,
            projected_ref,
            wide_t_ref,
            grad_attended_ref,
            mask_ref,
            lse_ref,
            dots_ref,
            grad_queries_t_ref,
            grad_projected_ref,
            grad_keys_ref,
            grad_values_ref,
        )

    grad_projected_ref[:, 0:width] = jnp.transpose(grad_queries_t_ref[...].astype(bf16))
    for at in range(0, length, ROW_CHUNK):
        norm, _ = normalized(tokens_ref[at : at + ROW_CHUNK].astype(f32))
        normed = (norm * row(GAIN1) + row(SHIFT1)).astype(bf16)
        wide_t_ref[:, at : at + ROW_CHUNK] = jnp.transpose(normed)
    small_ref[...] = small_in_ref[...]
    for part in range(3):
        columns = slice(part * width, (part + 1) * width)
        grad_part = grad_projected_ref[:, columns]
        grad_w_qkv_ref[:, columns] = matmul(wide_t_ref[...], grad_part, NN).astype(bf16)
        if part != 1:
            at = BIAS_Q if part == 0 else BIAS_V
            small_ref[at : at + 1, :] = total(grad_part.astype(f32))
    gain_sum = shift_sum = 0.0
    for at in range(0, length, ROW_CHUNK):
        rows = slice(at, at + ROW_CHUNK)
        grad_normed = matmul(grad_projected_ref[rows], w_qkv_ref[...], NT)
        norm, inverse = normalized(tokens_ref[rows].astype(f32))
        grad_rows = norm_pull(grad_normed, row(GAIN1), norm, inverse)
        grad_tokens_ref[rows] = (grad_middle_ref[rows] + grad_rows).astype(bf16)
        gain_sum = gain_sum + total(grad_normed * norm)
        shift_sum = shift_sum + total(grad_normed)
    small_ref[GAIN1 : GAIN1 + 1, :] = gain_sum
    small_ref[SHIFT1 : SHIFT1 + 1, :] = shift_sum


def kernel_params():
    return pltpu.CompilerParams(vmem_limit_bytes=VMEM_LIMIT)


def run_forward(tokens, segment, params, w_qkv):
    length, width = tokens.shape
    return pl.pallas_call(
        forward_kernel,
        in_specs=[WHOLE] * 4,
        out_specs=(WHOLE,) * 3,
        out_shape=(
            jax.ShapeDtypeStruct((length, 3 * width), bf16),
            jax.ShapeDtypeStruct((width, length), bf16),
            jax.ShapeDtypeStruct((16, length), f32),
        ),
        scratch_shapes=[
            pltpu.VMEM((length, length), f32),
            pltpu.VMEM((length, width), bf16),
            pltpu.VMEM((width, length), bf16),
        ],
        compiler_params=kernel_params(),
        name="forward",
    )(tokens, segment, params, w_qkv)


def run_hidden(attended_t, tokens, cotangent, params, w_out, w_fc, w_proj):
    length, width = tokens.shape
    hidden = w_fc.shape[1]
    shape = jax.ShapeDtypeStruct
    columns = pl.BlockSpec((width, width), lambda step: (0, step))
    return pl.pallas_call(
        hidden_kernel,
        grid=(hidden // width,),
        in_specs=[WHOLE] * 5 + [columns, pl.BlockSpec((width, width), lambda step: (step, 0))],
        out_specs=(WHOLE, WHOLE, WHOLE, WHOLE, columns, columns, WHOLE),
        out_shape=(
            shape((length, width), bf16),
            shape((length, width), f32),
            shape((length, width), bf16),
            shape((width, width), bf16),
            shape((width, hidden), bf16),
            shape((width, hidden), bf16),
            shape((16, width), f32),
        ),
        scratch_shapes=[
            pltpu.VMEM((length, width), f32),
            pltpu.VMEM((length, width), bf16),
            pltpu.VMEM((width, length), bf16),
            pltpu.VMEM((width, length), bf16),
            pltpu.VMEM((length, width), f32),
            pltpu.VMEM((length, width), f32),
            pltpu.VMEM((length, width), bf16),
            pltpu.VMEM((length, width), bf16),
        ],
        compiler_params=kernel_params(),
        name="hidden",
    )(attended_t, tokens, cotangent, params, w_out, w_fc, w_proj)


def run_backward(
    tokens, segment, params, w_qkv, projected, attended_t, lse, grad_attended, grad_middle, small
):
    length, width = tokens.shape
    shape = jax.ShapeDtypeStruct
    return pl.pallas_call(
        backward_kernel,
        in_specs=[WHOLE] * 10,
        out_specs=(WHOLE,) * 3,
        out_shape=(
            shape((length, width), bf16),
            shape((width, 3 * width), bf16),
            shape((16, width), f32),
        ),
        scratch_shapes=[
            pltpu.VMEM((length, length), f32),
            pltpu.VMEM((width, length), bf16),
            pltpu.VMEM((width, length), f32),
            pltpu.VMEM((16, length), f32),
            pltpu.VMEM((length, 3 * width), bf16),
            pltpu.VMEM((length, 2 * HEAD), f32),
            pltpu.VMEM((length, 2 * HEAD), f32),
        ],
        compiler_params=kernel_params(),
        name="backward",
    )(
        tokens,
        segment,
        params,
        w_qkv,
        projected,
        attended_t,
        lse,
        grad_attended,
        grad_middle,
        small,
    )


def on_device(
    tokens,
    segment_ids,
    norm1_gain,
    norm1_shift,
    w_qkv,
    q_bias,
    v_bias,
    w_out,
    out_bias,
    norm2_gain,
    norm2_shift,
    w_fc,
    fc_bias,
    w_proj,
    proj_bias,
    cotangent,
):
    width = tokens.shape[1]
    gather = partial(lax.all_gather, axis_name="shard", axis=0, tiled=True)
    vectors = (
        norm1_gain,
        norm1_shift,
        q_bias,
        v_bias,
        out_bias,
        norm2_gain,
        norm2_shift,
        proj_bias,
    )
    own = norm1_gain.shape[0]
    packed = jnp.concatenate(vectors + (fc_bias,))
    packed = lax.all_gather(packed, "shard", axis=0)
    rows = packed[:, : 8 * own].reshape(-1, 8, own).transpose(1, 0, 2).reshape(8, width)
    params = jnp.concatenate([rows, packed[:, 8 * own :].reshape(-1, width)]).astype(f32)
    params = jnp.pad(params, ((0, 16 - params.shape[0]), (0, 0)))
    full_qkv, full_out, full_fc, full_proj = (gather(w) for w in (w_qkv, w_out, w_fc, w_proj))
    projected, attended_t, lse = run_forward(tokens, segment_ids, params, full_qkv)
    (
        layer_out,
        grad_middle,
        grad_attended,
        grad_w_out,
        grad_w_fc,
        grad_w_proj_t,
        small,
    ) = run_hidden(attended_t, tokens, cotangent, params, full_out, full_fc, full_proj)
    grad_tokens, grad_w_qkv, small = run_backward(
        tokens,
        segment_ids,
        params,
        full_qkv,
        projected,
        attended_t,
        lse,
        grad_attended,
        grad_middle,
        small,
    )

    def reduced(grad, dim):
        mine = lax.psum_scatter(grad.astype(f32), "shard", scatter_dimension=dim, tiled=True)
        return lax.psum(mine.astype(bf16), "rep").astype(f32)

    sum_proj = reduced(grad_w_proj_t, 1).T
    sum_fc = reduced(grad_w_fc, 0)
    sum_out = reduced(grad_w_out, 0)
    sum_qkv = reduced(grad_w_qkv, 0)
    small = lax.psum(small, ("rep", "shard"))
    me = lax.axis_index("shard")
    mine = lax.dynamic_slice_in_dim(small[:8], me * own, own, 1)
    hidden_rows = small[BIAS_FC : BIAS_FC + w_fc.shape[1] // width].reshape(-1)
    mine_fc = lax.dynamic_slice_in_dim(hidden_rows, me * fc_bias.shape[0], fc_bias.shape[0], 0)
    return (
        layer_out,
        grad_tokens,
        mine[GAIN1],
        mine[SHIFT1],
        sum_qkv,
        mine[BIAS_Q],
        mine[BIAS_V],
        sum_out,
        mine[BIAS_OUT],
        mine[GAIN2],
        mine[SHIFT2],
        sum_fc,
        mine_fc,
        sum_proj,
        mine[BIAS_PROJ],
    )


def solution(mesh):
    rows, own, own_rows = P(("rep", "shard"), None), P("shard"), P("shard", None)
    in_specs = (
        rows,
        rows,
        own,
        own,
        own_rows,
        own,
        own,
        own_rows,
        own,
        own,
        own,
        own_rows,
        own,
        own_rows,
        own,
        rows,
    )
    out_specs = (
        rows,
        rows,
        own,
        own,
        own_rows,
        own,
        own,
        own_rows,
        own,
        own,
        own,
        own_rows,
        own,
        own_rows,
        own,
    )
    return jax.shard_map(
        on_device, mesh=mesh, in_specs=in_specs, out_specs=out_specs, check_vma=False
    )
```

time: 1030 us -> 819 us (0.80)
  matrix products: 246 us -> 0 us
  Pallas kernels: 0 us -> 130 us
  other arithmetic: 113 us -> 14 us
  waiting for transfers between devices: 499 us -> 583 us
  local copies, waits for them, and re-layouts: 46.3 us -> 2.94 us
  blocking collectives: 107 us -> 73.5 us
    dot_general x24 -> x0, matrix products: 246 us -> none  [the longest x2 39 us: attend_backward(): jnp.einsum('qhd,khd->hqk', g_block, value_rows, preferred_element_type=jn...]
    pallas_call x0 -> x3, Pallas kernels: none -> 130 us  [the longest x1 57.9 us: run_hidden(): pl.pallas_call(hidden_kernel, grid=(hidden // width,), in_specs=[WHOLE] *...]
    all_gather x4, waiting for transfers between devices: 78 us -> 207 us  [on_device(): gather(w)]
    unnamed x2 -> x0, blocking collectives: 75.1 us -> none
    convert_element_type x27 -> x4, other arithmetic: 65.6 us -> 11.3 us  [the longest x1 7.29 us: reduced(): grad.astype(f32)]
    reduce_scatter x4, waiting for transfers between devices: 419 us -> 365 us  [reduced(): lax.psum_scatter(grad.astype(f32), 'shard', scatter_dimension=dim, tiled=...]
    reduce_sum x11 -> x0, other arithmetic: 42.7 us -> none  [the longest x2 25.6 us: attend_forward(): row_total = jnp.sum(exp_terms, axis=-1, keepdims=True)]
    psum x1, blocking collectives: 5.73 us -> 40.9 us  [on_device(): small = lax.psum(small, ('rep', 'shard'))]
  transfers between devices with their start and end apart: 9 -> 9, of which waited for: 5 -> 9; matrix products, arithmetic and copies ran while one was open for 24% -> 1% of each run, Pallas kernels for 0% -> 9%
where the time goes in v1:
time: 819 us; the launch traced here: 818 us
  waiting for transfers between devices  583 us (71%)
  Pallas kernels  130 us (16%)
  blocking collectives  73.5 us (9%)
  between operations  14.3 us (2%)
  other arithmetic  14 us (2%)
    reduce_scatter x4, waiting for transfers between devices, reduced(): lax.psum_scatter(grad.astype(f32), 'shard', scatter_dimension=dim, tiled=...  365 us
    all_gather x4, waiting for transfers between devices, on_device(): gather(w)  207 us
    pallas_call x1, Pallas kernels, run_hidden(): pl.pallas_call(hidden_kernel, grid=(hidden // width,), in_specs=[WHOLE] *...  57.9 us
    psum x1, blocking collectives, on_device(): small = lax.psum(small, ('rep', 'shard'))  40.9 us
    pallas_call x1, Pallas kernels, run_backward(): pl.pallas_call(backward_kernel, in_specs=[WHOLE] * 10, out_specs=(WHOLE,)...  40.8 us
    all_gather x1, blocking collectives, on_device(): packed = lax.all_gather(packed, 'shard', axis=0)  32.6 us
    pallas_call x1, Pallas kernels, run_forward(): pl.pallas_call(forward_kernel, in_specs=[WHOLE] * 4, out_specs=(WHOLE,) *...  30.8 us
  transfers between devices with their start and end apart: 9, of which 9 were waited for; matrix products, arithmetic and copies ran while one was open for 1% of the time, Pallas kernels for 9%

profile of v1, /device:TPU:0, one launch (start us, length us, event | category | flops | bytes accessed | tf_op | source)
XLA Modules:
  0.0 817.8 jit_solution(4699568725671386542)
XLA Ops:
  7.3 0.7 all-gather.7.cloned.1.call-update
  8.1 0.7 all-gather.9.cloned.1.call-update
  8.8 0.7 all-gather.11.cloned.1.call-update
  9.5 0.5 all-gather.13.cloned.1.call-update
  10.2 0.1 concatenate.6
  10.3 32.6 %all-gather.1 = bf16[8,1,1152]{2,1,0:T(2,128)(2,1)S(1)} all-gather(bf16[1,1,1152]{2,1,0:T(2,128)(2,1)S(1)} %reshape.47), channel_id=2, replica_groups=mesh['rep'=4,'shard'=8] {'shard'}, dimensions={0}, use_global_device_ids=true | all-gather | bytes 20736 | tf_op jit(solution)/shard_map/all_gather | solution.py:464
  42.9 0.1 reshape.42
  43.0 0.1 reshape.43
  43.1 0.6 fusion.3.params_ref
  43.8 34.6 %all-gather.7.cloned.1.call-done.w_qkv_ref = bf16[768,2304]{1,0:T(8,128)(2,1)} async-done(((bf16[96,2304]{1,0:T(8,128)(2,1)}), bf16[768,2304]{1,0:T(8,128)(2,1)}) %all-gather.7.cloned.1.call-update) | async-done | bytes 3538960 | tf_op jit(solution)/shard_map/all_gather | solution.py:468
  78.4 30.8 %forward.1 = (bf16[1024,2304]{1,0:T(8,128)(2,1)}, bf16[768,1024]{1,0:T(8,128)(2,1)}, f32[16,1024]{1,0:T(8,128)}) custom-call(bf16[1024,768]{1,0:T(8,128)(2,1)} %tokens_ref.5, s32[1,1024]{1,0:T(1,128)} %segment_ref.3, f32[16,768]{1,0:T(8,128)} %fusion.3.params_ref, bf16[768,2304]{1,0:T(8,128)(2,1)} %all-gather.7.cloned.1.call-done.w_qkv_ref), custom_call_target="tpu_custom_call" | custom-call | tf_op jit(solution)/shard_map/forward/pallas_call | solution.py:340
  109.3 11.0 %all-gather.9.cloned.1.call-done.w_out_ref = bf16[768,768]{1,0:T(8,128)(2,1)} async-done(((bf16[96,768]{1,0:T(8,128)(2,1)}), bf16[768,768]{1,0:T(8,128)(2,1)}) %all-gather.9.cloned.1.call-update) | async-done | bytes 1179664 | tf_op jit(solution)/shard_map/all_gather | solution.py:468
  120.3 80.9 %all-gather.11.cloned.1.call-done.w_fc_ref = bf16[768,3072]{1,0:T(8,128)(2,1)} async-done(((bf16[96,3072]{1,0:T(8,128)(2,1)}), bf16[768,3072]{1,0:T(8,128)(2,1)}) %all-gather.11.cloned.1.call-update) | async-done | bytes 4718608 | tf_op jit(solution)/shard_map/all_gather | solution.py:468
  201.1 80.1 %all-gather.13.cloned.1.call-done.w_proj_ref = bf16[3072,768]{1,0:T(8,128)(2,1)} async-done(((bf16[384,768]{1,0:T(8,128)(2,1)}), bf16[3072,768]{1,0:T(8,128)(2,1)}) %all-gather.13.cloned.1.call-update) | async-done | bytes 4718608 | tf_op jit(solution)/shard_map/all_gather | solution.py:468
  281.2 57.9 %hidden.1 = (bf16[1024,768]{1,0:T(8,128)(2,1)}, f32[1024,768]{1,0:T(8,128)}, bf16[1024,768]{1,0:T(8,128)(2,1)}, bf16[768,768]{1,0:T(8,128)(2,1)}, bf16[768,3072]...) custom-call(bf16[768,1024]{1,0:T(8,128)(2,1)} %get-tuple-element.28.attended_t_ref, ...), custom_call_target="tpu_custom_call" | custom-call | tf_op jit(solution)/shard_map/hidden/pallas_call | solution.py:364
  339.1 7.3 convert_element_type.46
  346.5 0.5 reduce-scatter.7.cloned.1.call-update
  347.1 40.8 %backward.1 = (bf16[1024,768]{1,0:T(8,128)(2,1)}, bf16[768,2304]{1,0:T(8,128)(2,1)}, f32[16,768]{1,0:T(8,128)}) custom-call(bf16[1024,768]{1,0:T(8,128)(2,1)} %tokens_ref.5, s32[1,1024]{1,0:T(1,128)} %segment_ref.3, f32[16,768]{1,0:T(8,128)} %fusion.3.params_ref, bf16[768,2304]{1,0:T(8,128)(2,1)} %all-gather.7.cloned.1.call-done.w_qkv_ref, ...), custom_call_target="tpu_custom_call" | custom-call | tf_op jit(solution)/shard_map/backward/pallas_call | solution.py:398
  388.0 0.7 reduce-scatter.9.cloned.1.call-update
  388.7 119.5 %reduce-scatter.11.cloned.1.call-done = f32[768,384]{1,0:T(8,128)} async-done(((f32[768,3072]{1,0:T(8,128)}), f32[768,384]{1,0:T(8,128)}) %reduce-scatter.11.cloned.1.call-update) | async-done | bytes 1179664 | tf_op jit(solution)/shard_map/reduce_scatter | solution.py:493
  508.2 2.1 convert_bitcast_fusion
  510.4 64.9 %reduce-scatter.7.cloned.1.call-done = bf16[96,768]{1,0:T(8,128)(2,1)} async-done(((bf16[768,768]{1,0:T(8,128)(2,1)}), bf16[96,768]{1,0:T(8,128)(2,1)}) %reduce-scatter.7.cloned.1.call-update) | async-done | bytes 147472 | tf_op jit(solution)/shard_map/reduce_scatter | solution.py:493
  575.2 81.8 %reduce-scatter.5.cloned.1.call-done = bf16[96,2304]{1,0:T(8,128)(2,1)} async-done(((bf16[768,2304]{1,0:T(8,128)(2,1)}), bf16[96,2304]{1,0:T(8,128)(2,1)}) %reduce-scatter.5.cloned.1.call-update) | async-done | bytes 442384 | tf_op jit(solution)/shard_map/reduce_scatter | solution.py:493
  657.0 98.5 %reduce-scatter.9.cloned.1.call-done = bf16[96,3072]{1,0:T(8,128)(2,1)} async-done(((bf16[768,3072]{1,0:T(8,128)(2,1)}), bf16[96,3072]{1,0:T(8,128)(2,1)}) %reduce-scatter.9.cloned.1.call-update) | async-done | bytes 589840 | tf_op jit(solution)/shard_map/reduce_scatter | solution.py:493
  755.5 40.9 %psum.35 = f32[16,768]{1,0:T(8,128)S(1)} all-reduce(f32[16,768]{1,0:T(8,128)S(1)} %copy-done.3), channel_id=1, replica_groups=mesh['rep'=4,'shard'=8] {'rep','shard'}, use_global_device_ids=true, to_apply=%region_0.1 | all-reduce | flops 12288 | bytes 98304 | tf_op jit(solution)/shard_map/psum | solution.py:500
  796.5 0.7 dynamic_slice.7
  797.2 0.5 slice_bitcast_fusion
  797.7 8.1 all-reduce.4.cloned.1.call-done
  805.8 2.3 convert_element_type.45
  808.1 1.3 copy.36
  809.4 1.0 convert_element_type.39
  810.4 0.7 convert_element_type.42
  (48 shorter events, 0.6 us)
Async XLA Ops:
  7.2 2.9 copy-start.5
  7.2 2.9 copy-start.6
  7.2 2.9 copy-start.7
  7.2 2.9 copy-start.8
  7.2 2.9 copy-start.9
  7.2 2.9 copy-start.10
  7.2 2.9 copy-start.11
  7.3 2.9 copy-start.4
  7.3 2.9 copy-start.12
  7.3 71.1 %all-gather.7.cloned.1.call-start = ((), (), s32[]{:S(2)}) async-start(), calls=%async_computation.4 | async-start | bytes 3981312 | tf_op jit(solution)/shard_map/all_gather | solution.py:468
  8.0 112.3 %all-gather.9.cloned.1.call-start = ((), (), s32[]{:S(2)}) async-start(), calls=%async_computation.5 | async-start | bytes 1327104 | tf_op jit(solution)/shard_map/all_gather | solution.py:468
  8.8 192.4 %all-gather.11.cloned.1.call-start = ((), (), s32[]{:S(2)}) async-start(), calls=%async_computation.6 | async-start | bytes 5308416 | tf_op jit(solution)/shard_map/all_gather | solution.py:468
  9.5 271.7 %all-gather.13.cloned.1.call-start = ((), (), s32[]{:S(2)}) async-start(), calls=%async_computation.7 | async-start | bytes 5308416 | tf_op jit(solution)/shard_map/all_gather | solution.py:468
  10.1 498.1 %reduce-scatter.11.cloned.1.call-start = ((), (), s32[]{:S(2)}) async-start(), calls=%async_computation.11 | async-start | bytes 10616832 | tf_op jit(solution)/shard_map/reduce_scatter | solution.py:493
  346.4 228.8 %reduce-scatter.7.cloned.1.call-start = ((), (), s32[]{:S(2)}) async-start(), calls=%async_computation.9 | async-start | bytes 1327104 | tf_op jit(solution)/shard_map/reduce_scatter | solution.py:493
  347.0 310.0 %reduce-scatter.5.cloned.1.call-start = ((), (), s32[]{:S(2)}) async-start(), calls=%async_computation.8 | async-start | bytes 3981312 | tf_op jit(solution)/shard_map/reduce_scatter | solution.py:493
  387.9 367.5 %reduce-scatter.9.cloned.1.call-start = ((), (), s32[]{:S(2)}) async-start(), calls=%async_computation.10 | async-start | bytes 5308416 | tf_op jit(solution)/shard_map/reduce_scatter | solution.py:493
  388.7 366.8 %copy-start.3 = (f32[16,768]{1,0:T(8,128)S(1)}, f32[16,768]{1,0:T(8,128)}, u32[]{:S(2)}) copy-start(f32[16,768]{1,0:T(8,128)} %get-tuple-element.36) | copy-start | bytes 147460
  388.7 417.1 %all-reduce.4.cloned.1.call-start = ((), (), s32[]{:S(2)}) async-start(), calls=%async_computation.12 | async-start | bytes 3538944 | tf_op jit(solution)/shard_map/psum | solution.py:494
  805.8 2.3 copy-start
  805.8 3.5 copy-start.1
  808.1 2.3 copy-start.2
Sparse Core Ops, SparseCore 0:
  10.3 68.0 all-gather.6
  80.6 39.6 all-gather.8
  122.4 78.6 all-gather.10
  203.2 78.0 all-gather.12
  346.6 161.5 reduce-scatter.10
  512.0 63.1 reduce-scatter.6
  578.8 78.0 reduce-scatter.4
  660.6 94.8 reduce-scatter.8
  758.7 47.1 all-reduce.3
